TPU v7x, 512 devices: a whole 4x4x16 slice. The times are simulated.
512 devices in a mesh: kpt: 16 (over x, y_lo, core), aux: 32 (over z, y_hi).
Axes of the slice: x: 4, y: 4 (y_hi: 2, y_lo: 2; y = y_hi * 2 + y_lo), z: 16, core: 2. Of those that a mesh axis runs over, the one named last changes fastest.
Arguments:
- orbitals: bfloat16 [16, 768, 384], P('kpt', 'aux'), may hold values from -6 to 6
- fitted: bfloat16 [16, 2, 64, 768, 768], P('kpt', None, 'aux'), may hold values from -0.21875 to 0.21875
- kpoint_pair_index: int32 [16, 4], P('kpt'), may hold values from 0 to 1
Outputs:
- exchange_images: float32 [2, 16, 768, 384], P(None, 'kpt', 'aux')
- orbitals_out: float32 [16, 768, 384], P('kpt', 'aux')
Inputs may be any that keep to these rules, and one draw needn't show every extreme that they name: kpoint_pair_index[k, v] names which of the 2 fitted tensors of k-point k serves visit v.
All inputs are finite; a program needn't handle non-finite values.
Results may differ from a plain program's by a relative error of at most 0.0011.
Values may be sent and summed in bfloat16 or wider, within the bound.
A program may use at most 64 MiB of HBM per device.

v0:
```python
import jax
import jax.numpy as jnp
from jax import lax
from jax.sharding import PartitionSpec as P

VISIT_COUNT = 4
update_fraction = 0.25


def passed_along(value, axis, by):
    count = lax.axis_size(axis)
    return lax.ppermute(value, axis, [(i, (i + by) % count) for i in range(count)])


def half_transform(slot_block, paired_kpoint):
    layers = slot_block.shape[0]
    flattened = slot_block.reshape(layers * slot_block.shape[1], slot_block.shape[2])
    half_done = jnp.dot(flattened, paired_kpoint, preferred_element_type=jnp.float32).astype(
        jnp.bfloat16
    )
    return half_done.reshape(layers, slot_block.shape[1], paired_kpoint.shape[1])


def on_device(orbitals, fitted, kpoint_pair_index):
    rows_here = orbitals.shape[1]
    norm_scale = 1.0 / (fitted.shape[2] * lax.axis_size("aux") * orbitals.shape[2])
    current = orbitals[0].astype(jnp.float32)
    fitted_point = fitted[0]
    applied_list = []
    for outer in range(VISIT_COUNT // 2):
        offset = outer + 1
        rounded = current.astype(jnp.bfloat16)
        own_full = lax.all_gather(rounded, "aux", axis=0, tiled=True)
        trailing = passed_along(own_full, "kpt", offset)
        leading = passed_along(own_full, "kpt", -offset)
        slot_first = lax.dynamic_index_in_dim(
            fitted_point, kpoint_pair_index[0, 2 * outer], 0, keepdims=False
        )
        slot_second = lax.dynamic_index_in_dim(
            fitted_point, kpoint_pair_index[0, 2 * outer + 1], 0, keepdims=False
        )
        half_done = jnp.concatenate(
            (half_transform(slot_first, trailing), half_transform(slot_second, leading)), axis=0
        )
        inner_block = jnp.einsum(
            "pmi,mj->pij", half_done, own_full, preferred_element_type=jnp.float32
        ).astype(jnp.bfloat16)
        partial_sum = jnp.einsum(
            "pmi,pij->mj", half_done, inner_block, preferred_element_type=jnp.float32
        )
        summed = lax.psum(partial_sum, "aux")
        applied = lax.dynamic_slice_in_dim(summed, lax.axis_index("aux") * rows_here, rows_here, 0)
        applied = applied * norm_scale
        applied_list.append(applied)
        current = current - update_fraction * applied
    return (jnp.stack(applied_list)[:, None], current[None])


def solution(mesh):
    placed = (P("kpt", "aux", None), P("kpt", None, "aux", None, None), P("kpt", None))
    return jax.shard_map(
        on_device,
        mesh=mesh,
        in_specs=placed,
        out_specs=(P(None, "kpt", "aux", None), P("kpt", "aux", None)),
        check_vma=False,
    )
```

profile of v0, /device:TPU:6, one launch (start us, length us, event | category | flops | bytes accessed | tf_op | source)
XLA Modules:
  0.0 860.2 jit_solution(11143747537137993466)
XLA Ops:
  7.2 0.0 all-reduce.3.cloned.1.call-start
  7.2 86.2 %all-gather = bf16[1,768,384]{2,1,0:T(8,128)(2,1)S(1)} all-gather(bf16[1,24,384]{2,1,0:T(8,128)(2,1)} %param.3), channel_id=2, replica_groups=mesh['kpt'=16,'aux'=32] {'aux'}, dimensions={1}, use_global_device_ids=true | all-gather | bytes 608256 | tf_op jit(solution)/shard_map/all_gather | solution.py:33
  93.4 1.9 collective-permute-start
  95.3 4.5 collective-permute-start.1
  99.9 1.5 fusion.13
  109.1 5.9 constant_dynamic-slice_fusion.1
  115.0 0.0 collective-permute-done
  115.0 3.5 convolution_convert_fusion.3
  118.5 0.0 collective-permute-done.1
  118.5 3.5 convolution_convert_fusion.2
  122.0 0.0 copy-start
  122.0 6.1 fusion.2
  128.0 0.0 all-reduce.3.cloned.1.call-update
  128.0 0.0 all-reduce.5.cloned.1.call-start
  128.1 304.9 %all-reduce.3.cloned.1.call-done = f32[768,384]{1,0:T(8,128)} async-done(((f32[768,384]{1,0:T(8,128)}), f32[768,384]{1,0:T(8,128)}) %all-reduce.3.cloned.1.call-update) | async-done | bytes 1179664 | tf_op jit(solution)/shard_map/psum | solution.py:51
  433.0 0.0 copy-done
  433.0 0.8 fusion.8
  433.8 79.0 %all_gather.7 = bf16[768,384]{1,0:T(8,128)(2,1)S(1)} all-gather(bf16[24,384]{1,0:T(8,128)(2,1)S(1)} %fusion.8), channel_id=1, replica_groups=mesh['kpt'=16,'aux'=32] {'aux'}, dimensions={0}, use_global_device_ids=true | all-gather | bytes 608256 | tf_op jit(solution)/shard_map/all_gather | solution.py:33
  512.8 3.0 collective-permute-start.2
  515.7 3.7 collective-permute-start.3
  519.5 9.9 %collective-permute-done.2 = bf16[768,384]{1,0:T(8,128)(2,1)S(1)} collective-permute-done((bf16[768,384]{1,0:T(8,128)(2,1)S(1)}, bf16[768,384]{1,0:T(8,128)(2,1)S(1)}, u32[]{:S(2)}, u32[]{:S(2)}) %collective-permute-start.2) | collective-permute-done | bytes 589856 | tf_op jit(solution)/shard_map/ppermute | solution.py:12
  529.4 4.1 convolution_convert_fusion.1
  533.6 0.0 collective-permute-done.3
  533.6 2.5 convolution_convert_fusion
  536.0 6.0 fusion.3
  542.1 0.0 all-reduce.5.cloned.1.call-update
  542.1 309.2 %all-reduce.5.cloned.1.call-done = f32[768,384]{1,0:T(8,128)} async-done(((f32[768,384]{1,0:T(8,128)}), f32[768,384]{1,0:T(8,128)}) %all-reduce.5.cloned.1.call-update) | async-done | bytes 1179664 | tf_op jit(solution)/shard_map/psum | solution.py:51
  851.3 1.4 subtract_bitcast_fusion
  852.7 0.6 maximum_bitcast_fusion
Async XLA Ops:
  7.2 425.8 %all-reduce.3.cloned.1.call-start = ((), (), s32[]{:S(2)}) async-start(), calls=%async_computation | async-start | bytes 2359296 | tf_op jit(solution)/shard_map/psum | solution.py:51
  93.4 21.6 %collective-permute-start = (bf16[768,384]{1,0:T(8,128)(2,1)S(1)}, bf16[768,384]{1,0:T(8,128)(2,1)}, u32[]{:S(2)}, u32[]{:S(2)}) collective-permute-start(bf16[768,384]{1,0:T(8,128)(2,1)S(1)} %bitcast.51), channel_id=1, source_target_pairs={{0,32},{32,64},{64,96},{96,128},{128,160},{160,192},{192,224},{224... | collective-permute-start | bytes 1769480 | tf_op jit(solution)/shard_map/ppermute | solution.py:12
  95.3 23.1 %collective-permute-start.1 = (bf16[768,384]{1,0:T(8,128)(2,1)S(1)}, bf16[768,384]{1,0:T(8,128)(2,1)}, u32[]{:S(2)}, u32[]{:S(2)}) collective-permute-start(bf16[768,384]{1,0:T(8,128)(2,1)S(1)} %bitcast.52), channel_id=1, source_target_pairs={{0,480},{32,0},{64,32},{96,64},{128,96},{160,128},{192,160},{224,1... | collective-permute-start | bytes 1769480 | tf_op jit(solution)/shard_map/ppermute | solution.py:12
  122.0 311.0 %copy-start = (bf16[1,24,384]{2,1,0:T(8,128)(2,1)S(1)}, bf16[1,24,384]{2,1,0:T(8,128)(2,1)}, u32[]{:S(2)}) copy-start(bf16[1,24,384]{2,1,0:T(8,128)(2,1)} %param.3) | copy-start | bytes 55300
  128.0 723.3 %all-reduce.5.cloned.1.call-start = ((), (), s32[]{:S(2)}) async-start(), calls=%async_computation.1 | async-start | bytes 2359296 | tf_op jit(solution)/shard_map/psum | solution.py:51
  512.8 16.7 %collective-permute-start.2 = (bf16[768,384]{1,0:T(8,128)(2,1)S(1)}, bf16[768,384]{1,0:T(8,128)(2,1)S(1)}, u32[]{:S(2)}, u32[]{:S(2)}) collective-permute-start(bf16[768,384]{1,0:T(8,128)(2,1)S(1)} %all_gather.7), channel_id=1, source_target_pairs={{0,64},{32,96},{64,128},{96,160},{128,192},{160,224},{192,256},{22... | collective-permute-start | bytes 1769480 | tf_op jit(solution)/shard_map/ppermute | solution.py:12
  515.7 17.8 %collective-permute-start.3 = (bf16[768,384]{1,0:T(8,128)(2,1)S(1)}, bf16[768,384]{1,0:T(8,128)(2,1)S(1)}, u32[]{:S(2)}, u32[]{:S(2)}) collective-permute-start(bf16[768,384]{1,0:T(8,128)(2,1)S(1)} %all_gather.7), channel_id=1, source_target_pairs={{0,448},{32,480},{64,0},{96,32},{128,64},{160,96},{192,128},{224,1... | collective-permute-start | bytes 1769480 | tf_op jit(solution)/shard_map/ppermute | solution.py:12
Sparse Core Ops, SparseCore 0:
  128.2 304.7 all-reduce.2
  542.2 309.0 all-reduce.4
where the time goes:
time: 861 us; the launch traced here: 860 us
  waiting for transfers between devices  624 us (72%)
  blocking collectives  165 us (19%)
  matrix products  25.6 us (3%)
  between operations  21.8 us (3%)
  starting transfers between devices  13.3 us (2%)
    psum x2, waiting for transfers between devices, on_device(): summed = lax.psum(partial_sum, 'aux')  614 us
    all_gather x2, blocking collectives, on_device(): own_full = lax.all_gather(rounded, 'aux', axis=0, tiled=True)  165 us
  transfers between devices with their start and end apart: 6, of which 3 were waited for; matrix products, arithmetic and copies ran while one was open for 2% of the time, Pallas kernels for 0%

commit v1 on v0

--- a/solution.py
+++ b/solution.py
@@ -30,7 +30,9 @@
     for outer in range(VISIT_COUNT // 2):
         offset = outer + 1
         rounded = current.astype(jnp.bfloat16)
-        own_full = lax.all_gather(rounded, "aux", axis=0, tiled=True)
+        own_full = jnp.concatenate(
+            lax.all_to_all(jnp.stack([rounded] * lax.axis_size("aux")), "aux", 0, 0), axis=0
+        )
         trailing = passed_along(own_full, "kpt", offset)
         leading = passed_along(own_full, "kpt", -offset)
         slot_first = lax.dynamic_index_in_dim(

time: 861 us -> 777 us (0.902)
  blocking collectives: 165 us -> 88 us
    all_gather x2 -> x0, blocking collectives: 165 us -> none  [on_device(): own_full = lax.all_gather(rounded, 'aux', axis=0, tiled=True)]
    all_to_all x0 -> x2, blocking collectives: none -> 88 us  [on_device(): lax.all_to_all(jnp.stack([rounded] * lax.axis_size('aux')), 'aux', 0, 0)]
where the time goes in v1:
time: 777 us; the launch traced here: 776 us
  waiting for transfers between devices  617 us (79%)
  blocking collectives  88 us (11%)
  matrix products  24.6 us (3%)
  between operations  21.9 us (3%)
  starting transfers between devices  13.3 us (2%)
  local copies, waits for them, and re-layouts  8.19 us (1%)
    psum x2, waiting for transfers between devices, on_device(): summed = lax.psum(partial_sum, 'aux')  608 us
    all_to_all x2, blocking collectives, on_device(): lax.all_to_all(jnp.stack([rounded] * lax.axis_size('aux')), 'aux', 0, 0)  88 us
  transfers between devices with their start and end apart: 6, of which 3 were waited for; matrix products, arithmetic and copies ran while one was open for 2% of the time, Pallas kernels for 0%

profile of v1, /device:TPU:6, one launch (start us, length us, event | category | flops | bytes accessed | tf_op | source)
XLA Modules:
  0.0 776.2 jit_solution(11099411661791189887)
XLA Ops:
  7.2 0.0 all-reduce.3.cloned.1.call-start
  7.2 0.8 stack.13
  8.0 53.7 %all_to_all.10 = bf16[32,24,384]{2,1,0:T(8,128)(2,1)S(1)} all-to-all(bf16[32,24,384]{2,1,0:T(8,128)(2,1)S(1)} %stack.13), channel_id=1, replica_groups=mesh['kpt'=16,'aux'=32] {'aux'}, dimensions={0} | all-to-all | bytes 1179648 | tf_op jit(solution)/shard_map/all_to_all | solution.py:34
  61.7 1.9 collective-permute-start
  63.6 1.5 fusion.9
  72.9 4.5 collective-permute-start.1
  77.4 5.9 constant_dynamic-slice_fusion.1
  83.3 0.0 collective-permute-done
  83.3 3.5 convolution_convert_fusion.3
  86.8 0.0 collective-permute-done.1
  86.8 2.5 convolution_convert_fusion.2
  89.3 0.0 copy-start
  89.3 6.1 fusion.2
  95.4 0.0 all-reduce.3.cloned.1.call-update
  95.4 0.0 all-reduce.5.cloned.1.call-start
  95.5 303.8 %all-reduce.3.cloned.1.call-done = f32[768,384]{1,0:T(8,128)} async-done(((f32[768,384]{1,0:T(8,128)}), f32[768,384]{1,0:T(8,128)}) %all-reduce.3.cloned.1.call-update) | async-done | bytes 1179664 | tf_op jit(solution)/shard_map/psum | solution.py:53
  399.3 0.0 copy-done
  399.3 0.8 fusion.4
  400.1 0.1 stack.15
  400.1 34.2 %all_to_all.11 = bf16[32,24,384]{2,1,0:T(8,128)(2,1)S(1)} all-to-all(bf16[32,24,384]{2,1,0:T(8,128)(2,1)S(1)} %stack.15), channel_id=1, replica_groups=mesh['kpt'=16,'aux'=32] {'aux'}, dimensions={0} | all-to-all | bytes 1179648 | tf_op jit(solution)/shard_map/all_to_all | solution.py:34
  434.4 1.9 collective-permute-start.2
  436.3 4.8 collective-permute-start.3
  441.1 8.9 %collective-permute-done.2 = bf16[768,384]{1,0:T(8,128)(2,1)S(1)} collective-permute-done((bf16[768,384]{1,0:T(8,128)(2,1)S(1)}, bf16[768,384]{1,0:T(8,128)(2,1)S(1)}, u32[]{:S(2)}, u32[]{:S(2)}) %collective-permute-start.2) | collective-permute-done | bytes 589856 | tf_op jit(solution)/shard_map/ppermute | solution.py:12
  450.0 4.1 convolution_convert_fusion.1
  454.1 0.0 collective-permute-done.3
  454.1 2.5 convolution_convert_fusion
  456.5 6.0 fusion.3
  462.6 0.0 all-reduce.5.cloned.1.call-update
  462.6 304.7 %all-reduce.5.cloned.1.call-done = f32[768,384]{1,0:T(8,128)} async-done(((f32[768,384]{1,0:T(8,128)}), f32[768,384]{1,0:T(8,128)}) %all-reduce.5.cloned.1.call-update) | async-done | bytes 1179664 | tf_op jit(solution)/shard_map/psum | solution.py:53
  767.3 1.4 subtract_bitcast_fusion
  768.7 0.6 maximum_bitcast_fusion
Async XLA Ops:
  7.2 392.1 %all-reduce.3.cloned.1.call-start = ((), (), s32[]{:S(2)}) async-start(), calls=%async_computation.2 | async-start | bytes 2359296 | tf_op jit(solution)/shard_map/psum | solution.py:53
  61.7 21.6 %collective-permute-start = (bf16[768,384]{1,0:T(8,128)(2,1)S(1)}, bf16[768,384]{1,0:T(8,128)(2,1)}, u32[]{:S(2)}, u32[]{:S(2)}) collective-permute-start(bf16[768,384]{1,0:T(8,128)(2,1)S(1)} %bitcast.49), channel_id=1, source_target_pairs={{0,32},{32,64},{64,96},{96,128},{128,160},{160,192},{192,224},{224... | collective-permute-start | bytes 1769480 | tf_op jit(solution)/shard_map/ppermute | solution.py:12
  72.9 13.9 %collective-permute-start.1 = (bf16[768,384]{1,0:T(8,128)(2,1)S(1)}, bf16[768,384]{1,0:T(8,128)(2,1)S(1)}, u32[]{:S(2)}, u32[]{:S(2)}) collective-permute-start(bf16[768,384]{1,0:T(8,128)(2,1)S(1)} %bitcast.50), channel_id=1, source_target_pairs={{0,480},{32,0},{64,32},{96,64},{128,96},{160,128},{192,160},{224,1... | collective-permute-start | bytes 1769480 | tf_op jit(solution)/shard_map/ppermute | solution.py:12
  89.3 310.0 %copy-start = (bf16[1,24,384]{2,1,0:T(8,128)(2,1)S(1)}, bf16[1,24,384]{2,1,0:T(8,128)(2,1)}, u32[]{:S(2)}) copy-start(bf16[1,24,384]{2,1,0:T(8,128)(2,1)} %param.3) | copy-start | bytes 55300
  95.4 671.9 %all-reduce.5.cloned.1.call-start = ((), (), s32[]{:S(2)}) async-start(), calls=%async_computation.3 | async-start | bytes 2359296 | tf_op jit(solution)/shard_map/psum | solution.py:53
  434.4 15.6 %collective-permute-start.2 = (bf16[768,384]{1,0:T(8,128)(2,1)S(1)}, bf16[768,384]{1,0:T(8,128)(2,1)S(1)}, u32[]{:S(2)}, u32[]{:S(2)}) collective-permute-start(bf16[768,384]{1,0:T(8,128)(2,1)S(1)} %bitcast.52), channel_id=1, source_target_pairs={{0,64},{32,96},{64,128},{96,160},{128,192},{160,224},{192,256},{22... | collective-permute-start | bytes 1769480 | tf_op jit(solution)/shard_map/ppermute | solution.py:12
  436.3 17.8 %collective-permute-start.3 = (bf16[768,384]{1,0:T(8,128)(2,1)S(1)}, bf16[768,384]{1,0:T(8,128)(2,1)S(1)}, u32[]{:S(2)}, u32[]{:S(2)}) collective-permute-start(bf16[768,384]{1,0:T(8,128)(2,1)S(1)} %bitcast.53), channel_id=1, source_target_pairs={{0,448},{32,480},{64,0},{96,32},{128,64},{160,96},{192,128},{224,1... | collective-permute-start | bytes 1769480 | tf_op jit(solution)/shard_map/ppermute | solution.py:12
Sparse Core Ops, SparseCore 0:
  95.5 303.7 all-reduce.2
  462.7 304.5 all-reduce.4
